TPU v7x, 256 devices: a whole 4x4x8 slice. The times are simulated.
256 devices in a mesh: seq: 32 (over y, x, core), tensor: 8 (over z).
Axes of the slice: x: 4, y: 4, z: 8, core: 2. Of those that a mesh axis runs over, the one named last changes fastest.
Arguments:
- hidden: bfloat16 [8192, 3072], P('seq'), may hold values from -6 to 6
- attention_norm_gain: bfloat16 [3072], replicated, may hold values from 0.099609375 to 1.8984375
- query_key_value_weight: bfloat16 [3, 3072, 3072], P(None, None, 'tensor'), may hold values from -0.109375 to 0.109375
- output_weight: bfloat16 [3072, 3072], P('tensor'), may hold values from -0.3125 to 0.3125
- adapter_down_weight: bfloat16 [3072, 16], P('tensor'), may hold values from -0.3125 to 0.3125
- adapter_up_weight: bfloat16 [16, 3072], replicated, may hold values from -1.5 to 1.5
- final_norm_gain: bfloat16 [3072], replicated, may hold values from 0.099609375 to 1.8984375
- head: bfloat16 [16384, 3072], P('tensor', 'seq')
- prompt_key_slots: bfloat16 [64, 128, 3072], P('seq', None, 'tensor')
- prompt_value_slots: bfloat16 [64, 128, 3072], P('seq', None, 'tensor'), may hold values from -6 to 6
- counts: int32 [8], replicated, may hold values from 1 to 8, as said below
- page_slot_index: int32 [64], replicated, may hold values from 0 to 63, each once
- owner: int32 [128], replicated, may hold values from 0 to 7, as said below
- targets: int32 [8192], P('seq'), may hold values from 0 to 16383
Outputs:
- logprob_policy: float32 [8192], P('seq')
- logprob_reference: float32 [8192], P('seq')
Inputs may be any that keep to these rules, and one draw needn't show every extreme that they name: `counts`: every prompt fills 1 to 8 pages, and some prompt fills exactly 8. `page_slot_index`: slot s is held by index s // 2 of seq; every slot is named once. `owner`: every prompt owns exactly 16 rollouts, placed anywhere.
All inputs are finite; a program needn't handle non-finite values.
Results may differ from a plain program's by a relative error of at most 0.014.
The roundings to bfloat16 on the way count: a program that leaves them out, or rounds other values in their place, can miss the bound.
Values may be sent and summed in bfloat16 or wider, within the bound.
No kernel may reach another device: no remote copies, remote signals or barrier semaphores. Data moves between devices by JAX's collectives and lax.ppermute only.
A program may use at most 192 MiB of HBM per device.

v0:
```python
import math
import jax
import jax.numpy as jnp
from jax import lax
from jax.sharding import PartitionSpec as P

HEAD_WIDTH = 96
LEN = 64
PAGE = 128
MAXP = 8
EPSILON = 1e-05
NEGATIVE = -1e30


def rms_norm(values, gain):
    mean_sq = jnp.mean(values * values, axis=-1, keepdims=True)
    return (values * lax.rsqrt(mean_sq + EPSILON) * gain.astype(jnp.float32)).astype(jnp.bfloat16)


def rotate(values, positions):
    half_width = values.shape[-1] // 2
    frequency = 10000.0 ** (-jnp.arange(half_width, dtype=jnp.float32) * 2.0 / values.shape[-1])
    angles = positions.astype(jnp.float32)[:, None] * frequency[None, :]
    cosine = jnp.cos(angles)[:, None, :]
    sinus = jnp.sin(angles)[:, None, :]
    first = values[..., :half_width]
    second = values[..., half_width:]
    return jnp.concatenate(
        [first * cosine - second * sinus, second * cosine + first * sinus], axis=-1
    )


def local(
    hidden,
    attention_norm_gain,
    query_key_value_weight,
    output_weight,
    adapter_down_weight,
    adapter_up_weight,
    final_norm_gain,
    head,
    prompt_key_slots,
    prompt_value_slots,
    counts,
    page_slot_index,
    owner,
    targets,
):
    tok_rows = hidden.shape[0]
    rollouts_here = tok_rows // LEN
    heads_here = output_weight.shape[0] // HEAD_WIDTH
    width_here = heads_here * HEAD_WIDTH
    score_scale = 1.0 / math.sqrt(HEAD_WIDTH)
    stream = hidden.astype(jnp.float32)
    normed = rms_norm(stream, attention_norm_gain)
    groups_iota = jnp.arange(counts.shape[0], dtype=jnp.int32)
    my_groups = lax.dynamic_slice_in_dim(
        owner, lax.axis_index("seq") * rollouts_here, rollouts_here, 0
    )
    tok_group = jnp.repeat(my_groups, LEN)
    group_pages = jnp.sum(
        jnp.where(tok_group[:, None] == groups_iota[None, :], counts[None, :], 0), axis=1
    )
    positions = group_pages * PAGE + jnp.arange(tok_rows, dtype=jnp.int32) % LEN
    queries = rotate(
        jnp.dot(normed, query_key_value_weight[0], preferred_element_type=jnp.float32).reshape(
            tok_rows, heads_here, HEAD_WIDTH
        ),
        positions,
    ).astype(jnp.bfloat16)
    keys_new = rotate(
        jnp.dot(normed, query_key_value_weight[1], preferred_element_type=jnp.float32).reshape(
            tok_rows, heads_here, HEAD_WIDTH
        ),
        positions,
    ).astype(jnp.bfloat16)
    values_new = (
        jnp.dot(normed, query_key_value_weight[2], preferred_element_type=jnp.float32)
        .astype(jnp.bfloat16)
        .reshape(tok_rows, heads_here, HEAD_WIDTH)
    )
    query_roll = queries.reshape(rollouts_here, LEN, heads_here, HEAD_WIDTH)
    key_roll = keys_new.reshape(rollouts_here, LEN, heads_here, HEAD_WIDTH)
    value_roll = values_new.reshape(rollouts_here, LEN, heads_here, HEAD_WIDTH)
    causal = jnp.arange(LEN, dtype=jnp.int32)[None, :] <= jnp.arange(LEN, dtype=jnp.int32)[:, None]
    own_scores = (
        jnp.einsum("rthd,rkhd->rhtk", query_roll, key_roll, preferred_element_type=jnp.float32)
        * score_scale
    )
    own_max = jnp.max(jnp.where(causal, own_scores, NEGATIVE), axis=-1)
    own_weights = jnp.where(causal, jnp.exp(own_scores - own_max[..., None]), 0.0)
    own_total = jnp.sum(own_weights, axis=-1)
    own_summed = jnp.einsum(
        "rhtk,rkhd->rhtd",
        own_weights.astype(jnp.bfloat16),
        value_roll,
        preferred_element_type=jnp.float32,
    )
    start_max = jnp.transpose(own_max, (1, 0, 2)).reshape(heads_here, tok_rows)
    start_total = jnp.transpose(own_total, (1, 0, 2)).reshape(heads_here, tok_rows)
    start_summed = jnp.transpose(own_summed, (1, 0, 2, 3)).reshape(heads_here, tok_rows, HEAD_WIDTH)
    entries = jnp.arange(page_slot_index.shape[0], dtype=jnp.int32)
    key_piece = lax.all_gather(prompt_key_slots, "seq", axis=0, tiled=True)
    value_piece = lax.all_gather(prompt_value_slots, "seq", axis=0, tiled=True)
    piece_slots = key_piece.shape[0]
    slot_ids = jnp.arange(piece_slots, dtype=jnp.int32)
    matches = page_slot_index[None, :] == slot_ids[:, None]
    slot_group = jnp.sum(jnp.where(matches, entries // MAXP, 0), axis=1)
    slot_page = jnp.sum(jnp.where(matches, entries % MAXP, 0), axis=1)
    slot_count = jnp.sum(
        jnp.where(slot_group[:, None] == groups_iota[None, :], counts[None, :], 0), axis=1
    )
    key_live = jnp.repeat(slot_page < slot_count, PAGE)
    key_group = jnp.repeat(slot_group, PAGE)
    visible = (tok_group[:, None] == key_group[None, :]) & key_live[None, :]
    totals = start_total
    summed = start_summed
    keys_flat = key_piece.reshape(piece_slots * PAGE, heads_here, HEAD_WIDTH)
    values_flat = value_piece.reshape(piece_slots * PAGE, heads_here, HEAD_WIDTH)
    scores = (
        jnp.einsum("thd,khd->htk", queries, keys_flat, preferred_element_type=jnp.float32)
        * score_scale
    )
    block_max = jnp.max(jnp.where(visible[None], scores, NEGATIVE), axis=-1)
    new_max = jnp.maximum(start_max, block_max)
    weights = jnp.where(visible[None], jnp.exp(scores - new_max[..., None]), 0.0)
    rescale = jnp.exp(start_max - new_max)
    totals = totals * rescale + jnp.sum(weights, axis=-1)
    summed = summed * rescale[..., None] + jnp.einsum(
        "htk,khd->htd",
        weights.astype(jnp.bfloat16),
        values_flat,
        preferred_element_type=jnp.float32,
    )
    attention_output = (summed / totals[..., None]).astype(jnp.bfloat16)
    attention_output = jnp.transpose(attention_output, (1, 0, 2)).reshape(tok_rows, width_here)
    branch_part = jnp.dot(attention_output, output_weight, preferred_element_type=jnp.float32)
    adapter_portion = jnp.dot(
        attention_output, adapter_down_weight, preferred_element_type=jnp.float32
    )
    branch_sum, adapter_delta = (
        lax.psum(branch_part.astype(jnp.bfloat16), "tensor").astype(jnp.float32),
        lax.psum(adapter_portion.astype(jnp.bfloat16), "tensor").astype(jnp.float32),
    )
    reference_hidden = stream + branch_sum
    policy_hidden = reference_hidden + jnp.dot(
        adapter_delta, adapter_up_weight.astype(jnp.float32), precision=lax.Precision.HIGHEST
    )
    normed_ref = rms_norm(reference_hidden, final_norm_gain)
    normed_pol = rms_norm(policy_hidden, final_norm_gain)
    head_rows = lax.all_gather(head, "seq", axis=1, tiled=True)
    stacked = jnp.concatenate([normed_pol, normed_ref], axis=0)
    logits = lax.dot_general(
        stacked, head_rows, (((1,), (1,)), ((), ())), preferred_element_type=jnp.float32
    )
    vocab_here = head_rows.shape[0]
    target_ids = jnp.concatenate([targets, targets], axis=0) - lax.axis_index("tensor") * vocab_here
    is_target = jnp.arange(vocab_here, dtype=jnp.int32)[None, :] == target_ids[:, None]
    picked = jnp.sum(jnp.where(is_target, logits, 0.0), axis=1)
    local_max = jnp.max(logits, axis=1)
    whole_max = lax.pmax(local_max, "tensor")
    local_total = jnp.sum(jnp.exp(logits - whole_max[:, None]), axis=1)
    whole_total, whole_picked = lax.psum((local_total, picked), "tensor")
    log_probs = whole_picked - whole_max - jnp.log(whole_total)
    return (log_probs[:tok_rows], log_probs[tok_rows:])


def solution(mesh):
    return jax.shard_map(
        local,
        mesh=mesh,
        in_specs=(
            P("seq", None),
            P(),
            P(None, None, "tensor"),
            P("tensor", None),
            P("tensor", None),
            P(),
            P(),
            P("tensor", "seq"),
            P("seq", None, "tensor"),
            P("seq", None, "tensor"),
            P(),
            P(),
            P(),
            P("seq"),
        ),
        out_specs=(P("seq"), P("seq")),
        check_vma=False,
    )
```

profile of v0, /device:TPU:2, one launch (start us, length us, event | category | flops | bytes accessed | tf_op | source)
XLA Modules:
  0.0 396.3 jit_solution(10816526754883917571)
XLA Ops:
  7.2 0.0 all-gather.4.cloned.1.call-start
  7.2 0.7 all-gather.4.cloned.1.call-update
  7.9 0.0 all-gather.6.cloned.1.call-start
  8.0 0.7 all-gather.6.cloned.1.call-update
  8.7 0.0 all-reduce.3.cloned.1.call-start
  8.7 0.7 dynamic_slice.3
  9.4 0.1 broadcast_in_dim.114
  9.5 0.1 eq.78
  9.6 0.7 convert_element_type.55
  10.3 5.1 %slice_bitcast_fusion = (bf16[384,3072]{0,1:T(8,128)(2,1)}, bf16[384,3072]{0,1:T(8,128)(2,1)}) fusion(bf16[3,3072,384]{2,1,0:T(8,128)(2,1)} %param.16), kind=kLoop, calls=%fused_computation.29 | loop fusion | bytes 9437184 | tf_op jit(solution)/shard_map/dot_general | solution.py:72
  15.4 4.3 %copy.69 = bf16[384,3072]{1,0:T(8,128)(2,1)} copy(bf16[384,3072]{0,1:T(8,128)(2,1)} %get-tuple-element.10) | data formatting | bytes 4718592 | tf_op jit(solution)/shard_map/dot_general | solution.py:72
  19.7 4.3 %copy.66 = bf16[384,3072]{1,0:T(8,128)(2,1)} copy(bf16[384,3072]{0,1:T(8,128)(2,1)} %get-tuple-element.11) | data formatting | bytes 4718592 | tf_op jit(solution)/shard_map/dot_general | solution.py:66
  24.0 0.1 select_reduce_fusion.5
  24.1 1.8 fusion.5
  25.9 0.3 multiply_cosine_fusion
  26.2 3.2 fusion.15
  29.4 0.1 copy-done.5
  29.6 0.9 fusion.17
  30.5 0.1 subtract_convert_fusion
  30.6 0.1 concatenate.32
  30.7 0.2 copy.67
  31.0 0.1 concatenate.33
  31.1 0.2 copy.68
  31.3 0.1 concatenate.35
  31.5 0.9 copy.70
  32.4 0.1 concatenate.36
  32.5 0.9 copy.71
  33.4 1.5 select_reduce_fusion.2
  34.9 0.1 fusion.31
  35.0 0.1 reshape.237
  35.1 0.1 reshape.234
  35.2 3.2 fusion.22
  38.4 0.2 reshape_reshape.3
  38.6 0.3 convolution_bitcast_fusion
  38.9 0.2 copy.77
  39.1 0.1 select_reduce_fusion.3
  39.2 0.1 select_reduce_fusion.6
  39.3 0.1 broadcast_bitcast_fusion.1
  39.4 0.1 broadcast_bitcast_fusion
  39.5 2.8 compare_and_fusion
  42.3 24.7 %all-gather.4.cloned.1.call-done = bf16[64,128,384]{2,1,0:T(8,128)(2,1)} async-done(((bf16[2,128,384]{2,1,0:T(8,128)(2,1)}), bf16[64,128,384]{2,1,0:T(8,128)(2,1)}) %all-gather.4.cloned.1.call-update) | async-done | bytes 6291472 | tf_op jit(solution)/shard_map/all_gather | solution.py:103
  67.0 9.0 %copy.76 = bf16[64,128,384]{1,0,2:T(8,128)(2,1)} copy(bf16[64,128,384]{2,1,0:T(8,128)(2,1)} %all-gather.4.cloned.1.call-done) | data formatting | bytes 12582912 | tf_op jit(solution)/shard_map/all_gather | solution.py:103
  76.0 10.3 %reshape.235 = bf16[8192,4,96]{0,2,1:T(8,128)(2,1)} reshape(bf16[64,128,384]{1,0,2:T(8,128)(2,1)} %copy.76) | data formatting | bytes 12582912 | tf_op jit(solution)/shard_map/reshape | solution.py:118
  86.3 36.4 %all-gather.6.cloned.1.call-done = bf16[64,128,384]{2,1,0:T(8,128)(2,1)} async-done(((bf16[2,128,384]{2,1,0:T(8,128)(2,1)}), bf16[64,128,384]{2,1,0:T(8,128)(2,1)}) %all-gather.6.cloned.1.call-update) | async-done | bytes 6291472 | tf_op jit(solution)/shard_map/all_gather | solution.py:104
  122.7 9.1 %copy.78 = bf16[64,128,384]{1,0,2:T(8,128)(2,1)} copy(bf16[64,128,384]{2,1,0:T(8,128)(2,1)} %all-gather.6.cloned.1.call-done) | data formatting | bytes 12582912 | tf_op jit(solution)/shard_map/all_gather | solution.py:104
  131.8 10.3 %reshape.236 = bf16[8192,4,96]{0,2,1:T(8,128)(2,1)} reshape(bf16[64,128,384]{1,0,2:T(8,128)(2,1)} %copy.78) | data formatting | bytes 12582912 | tf_op jit(solution)/shard_map/reshape | solution.py:119
  142.1 18.0 %select_reduce_fusion = (f32[4,256]{1,0:T(4,128)S(1)}, f32[4,256,8192]{2,1,0:T(8,128)}) fusion(pred[256,8192]{1,0:T(8,128)(4,1)} %compare_and_fusion, bf16[8192,4,96]{0,2,1:T(8,128)(2,1)} %reshape.235, bf16[256,4,48]{0,2,1:T(8,128)(2,1)S(1)} %get-tuple-element.16, bf16[256,4,48]{0,2,1:T(8,128)(2,1)S(1)} %copy-done.7), kind=kOutput, calls=%fused_computation.1 | convolution fusion | flops 1636170752 | bytes 42143744 | tf_op jit(solution)/shard_map/thd,khd->htk/dot_general | solution.py:121
  160.1 15.2 %fusion = f32[4,256]{1,0:T(4,128)S(1)} fusion(f32[4,256,8192]{2,1,0:T(8,128)} %get-tuple-element.27, f32[4,256]{1,0:T(4,128)S(1)} %max.15, pred[256,8192]{1,0:T(8,128)(4,1)S(1)} %copy-done.4), kind=kLoop, calls=%fused_computation.2 | loop fusion | flops 33553408 | bytes 35659776 | tf_op jit(solution)/shard_map/reduce_sum | solution.py:128
  175.4 15.2 %fusion.28 = bf16[4,256,96]{1,2,0:T(8,128)(2,1)S(1)} fusion(bf16[8192,4,96]{0,2,1:T(8,128)(2,1)} %reshape.236, f32[4,256,8192]{2,1,0:T(8,128)} %get-tuple-element.27, f32[4,256]{1,0:T(4,128)S(1)} %max.15, pred[256,8192]{1,0:T(8,128)(4,1)S(1)} %copy-done.4, f32[4,256,96]{1,2,0:T(8,128)S(1)} %copy.77, f32[4,256]{1,0:T(4,128)S(1)} %get-tuple-element.8, ...), kind=kOutput, calls=%fused_computation.40 | convolution fusion | flops 1644560384 | bytes 42545152 | tf_op jit(solution)/shard_map/htk,khd->htd/dot_general | solution.py:129
  190.7 2.1 convolution_convert_fusion
  192.8 0.0 all-gather.8.cloned.1.call-start
  192.9 0.5 all-gather.8.cloned.1.call-update
  193.5 0.1 convolution_convert_fusion.1
  193.6 17.8 %psum.29 = bf16[256,16]{0,1:T(8,128)(2,1)S(1)} all-reduce(bf16[256,16]{0,1:T(8,128)(2,1)S(1)} %convolution_convert_fusion.1), channel_id=1, replica_groups=mesh['seq'=32,'tensor'=8] {'tensor'}, use_global_device_ids=true, to_apply=%region_10.11 | all-reduce | flops 4096 | bytes 16384 | tf_op jit(solution)/shard_map/psum | solution.py:143
  211.4 60.1 %all-reduce.3.cloned.1.call-done = bf16[256,3072]{1,0:T(8,128)(2,1)} async-done(((bf16[256,3072]{1,0:T(8,128)(2,1)}), bf16[256,3072]{1,0:T(8,128)(2,1)}) %all-reduce.3.cloned.1.call-update) | async-done | bytes 1572880 | tf_op jit(solution)/shard_map/psum | solution.py:142
  271.6 2.9 multiply_reduce_fusion.1
  274.5 0.6 multiply_reduce_fusion
  275.1 3.0 multiply_convert_fusion.1
  278.1 63.1 %all-gather.8.cloned.1.call-done = bf16[2048,3072]{0,1:T(8,128)(2,1)} async-done(((bf16[2048,96]{0,1:T(8,128)(2,1)}), bf16[2048,3072]{0,1:T(8,128)(2,1)}) %all-gather.8.cloned.1.call-update) | async-done | bytes 12582928 | tf_op jit(solution)/shard_map/all_gather | solution.py:151
  341.2 11.9 %fusion.60 = (f32[512]{0:T(512)S(1)}, f32[512,2048]{1,0:T(8,128)}) fusion(bf16[2048,3072]{0,1:T(8,128)(2,1)} %all-gather.8.cloned.1.call-done, bf16[256,3072]{1,0:T(8,128)(2,1)} %get-tuple-element.19, bf16[256,3072]{1,0:T(8,128)(2,1)} %get-tuple-element.18), kind=kOutput, calls=%fused_computation.99 | convolution fusion | flops 6449790464 | bytes 19924992 | tf_op jit(solution)/shard_map/dot_general | solution.py:153
  353.1 17.4 %pmax.7 = f32[512]{0:T(512)S(1)} all-reduce(f32[512]{0:T(512)S(1)} %get-tuple-element.30), channel_id=1, replica_groups=mesh['seq'=32,'tensor'=8] {'tensor'}, use_global_device_ids=true, to_apply=%region_16.17 | all-reduce | flops 512 | bytes 4096 | tf_op jit(solution)/shard_map/pmax | solution.py:161
  370.5 3.6 select_reduce_fusion.1
  374.1 15.0 %all-reduce = (f32[512]{0:T(512)S(1)}, f32[512]{0:T(512)S(1)}) all-reduce(f32[512]{0:T(512)S(1)} %get-tuple-element.3, f32[512]{0:T(512)S(1)} %get-tuple-element.2), channel_id=1, replica_groups=mesh['seq'=32,'tensor'=8] {'tensor'}, use_global_device_ids=true, to_apply=%region_18.19 | all-reduce | flops 1024 | bytes 8192 | tf_op jit(solution)/shard_map/psum | solution.py:163
  389.2 0.6 fusion.59
  (44 shorter events, 0.2 us)
Async XLA Ops:
  7.2 183.5 %copy-start = (bf16[384,3072]{1,0:T(8,128)(2,1)S(1)}, bf16[384,3072]{1,0:T(8,128)(2,1)}, u32[]{:S(2)}) copy-start(bf16[384,3072]{1,0:T(8,128)(2,1)} %param.17) | copy-start | bytes 7077892
  7.2 59.8 %all-gather.4.cloned.1.call-start = ((), (), s32[]{:S(2)}) async-start(), calls=%async_computation | async-start | bytes 6488064 | tf_op jit(solution)/shard_map/all_gather | solution.py:103
  7.9 114.8 %all-gather.6.cloned.1.call-start = ((), (), s32[]{:S(2)}) async-start(), calls=%async_computation.1 | async-start | bytes 6488064 | tf_op jit(solution)/shard_map/all_gather | solution.py:104
  8.7 262.9 %all-reduce.3.cloned.1.call-start = ((), (), s32[]{:S(2)}) async-start(), calls=%async_computation.2 | async-start | bytes 3145728 | tf_op jit(solution)/shard_map/psum | solution.py:142
  19.7 4.3 %copy-start.13 = (s32[8]{0:T(128)S(1)}, s32[8]{0:T(128)}, u32[]{:S(2)}) copy-start(s32[8]{0:T(128)} %param.24) | copy-start | bytes 100
  26.2 3.3 copy-start.1
  26.2 3.4 copy-start.5
  30.6 2.8 copy-start.6
  38.4 0.7 copy-start.12
  131.8 10.3 %copy-start.7 = (bf16[256,4,48]{0,2,1:T(8,128)(2,1)S(1)}, bf16[256,4,48]{0,2,1:T(8,128)(2,1)}, u32[]{:S(2)}) copy-start(bf16[256,4,48]{0,2,1:T(8,128)(2,1)} %copy-done.6) | copy-start | bytes 294916
  142.1 18.0 %copy-start.4 = (pred[256,8192]{1,0:T(8,128)(4,1)S(1)}, pred[256,8192]{1,0:T(8,128)(4,1)}, u32[]{:S(2)}) copy-start(pred[256,8192]{1,0:T(8,128)(4,1)} %compare_and_fusion) | copy-start | bytes 6291460
  190.6 2.8 copy-start.10
  190.6 2.8 copy-start.11
  190.6 2.8 copy-start.9
  190.7 80.9 %copy-start.8 = (bf16[16,3072]{1,0:T(8,128)(2,1)S(1)}, bf16[16,3072]{1,0:T(8,128)(2,1)}, u32[]{:S(2)}) copy-start(bf16[16,3072]{1,0:T(8,128)(2,1)} %param.19) | copy-start | bytes 294916
  192.8 148.3 %all-gather.8.cloned.1.call-start = ((), (), s32[]{:S(2)}) async-start(), calls=%async_computation.3 | async-start | bytes 12976128 | tf_op jit(solution)/shard_map/all_gather | solution.py:151
  271.6 2.9 copy-start.2
  271.6 2.9 copy-start.3
Sparse Core Ops, SparseCore 0:
  10.6 56.3 all-gather.3
  69.5 53.1 all-gather.5
  193.0 78.5 all-reduce.2
  274.0 67.1 all-gather.7
where the time goes:
time: 398 us; the launch traced here: 396 us
  waiting for transfers between devices  186 us (47%)
  matrix products  59.3 us (15%)
  local copies, waits for them, and re-layouts  57.6 us (14%)
  blocking collectives  50.3 us (13%)
  other arithmetic  28.6 us (7%)
  between operations  14.1 us (4%)
    all_gather x1, waiting for transfers between devices, local(): head_rows = lax.all_gather(head, 'seq', axis=1, tiled=True)  63.1 us
    psum x1, waiting for transfers between devices, local(): lax.psum(branch_part.astype(jnp.bfloat16), 'tensor').astype(jnp.float32)  60.1 us
    all_gather x1, waiting for transfers between devices, local(): value_piece = lax.all_gather(prompt_value_slots, 'seq', axis=0, tiled=True)  36.4 us
    all_gather x1, waiting for transfers between devices, local(): key_piece = lax.all_gather(prompt_key_slots, 'seq', axis=0, tiled=True)  24.7 us
    dot_general x1, matrix products, local(): jnp.einsum('thd,khd->htk', queries, keys_flat, preferred_element_type=jnp...  18 us
    psum x1, blocking collectives, local(): lax.psum(adapter_portion.astype(jnp.bfloat16), 'tensor').astype(jnp.float32)  17.8 us
    pmax x1, blocking collectives, local(): whole_max = lax.pmax(local_max, 'tensor')  17.4 us
    reduce_sum x1, other arithmetic, local(): totals = totals * rescale + jnp.sum(weights, axis=-1)  15.2 us
  transfers between devices with their start and end apart: 4, of which 4 were waited for; matrix products, arithmetic and copies ran while one was open for 15% of the time, Pallas kernels for 0%

commit v1 on v0

--- a/solution.py
+++ b/solution.py
@@ -3,6 +3,7 @@
 import jax.numpy as jnp
 from jax import lax
 from jax.sharding import PartitionSpec as P
+from jax.lax import all_gather
 
 HEAD_WIDTH = 96
 LEN = 64
@@ -138,8 +139,9 @@
     adapter_portion = jnp.dot(
         attention_output, adapter_down_weight, preferred_element_type=jnp.float32
     )
+    _wrap_rounds = lambda s0: all_gather(s0, "tensor").sum(axis=0)
     branch_sum, adapter_delta = (
-        lax.psum(branch_part.astype(jnp.bfloat16), "tensor").astype(jnp.float32),
+        _wrap_rounds(branch_part.astype(jnp.bfloat16)).astype(jnp.float32),
         lax.psum(adapter_portion.astype(jnp.bfloat16), "tensor").astype(jnp.float32),
     )
     reference_hidden = stream + branch_sum

time: 398 us -> 452 us (1.14)
  waiting for transfers between devices: 186 us -> 231 us
  other arithmetic: 28.6 us -> 37.5 us
    all_gather x0 -> x1, waiting for transfers between devices: none -> 115 us  [local(): _wrap_rounds = lambda s0: all_gather(s0, 'tensor').sum(axis=0)]
    psum x1 -> x0, waiting for transfers between devices: 60.1 us -> none  [local(): lax.psum(branch_part.astype(jnp.bfloat16), 'tensor').astype(jnp.float32)]
    all_gather x1, waiting for transfers between devices: 63.1 us -> 53.4 us  [local(): head_rows = lax.all_gather(head, 'seq', axis=1, tiled=True)]
    reduce_sum x0 -> x1, other arithmetic: none -> 8.81 us  [local(): _wrap_rounds = lambda s0: all_gather(s0, 'tensor').sum(axis=0)]
where the time goes in v1:
time: 452 us; the launch traced here: 450 us
  waiting for transfers between devices  231 us (51%)
  matrix products  59.4 us (13%)
  local copies, waits for them, and re-layouts  57.6 us (13%)
  blocking collectives  50.7 us (11%)
  other arithmetic  37.5 us (8%)
  between operations  14.1 us (3%)
    all_gather x1, waiting for transfers between devices, local(): _wrap_rounds = lambda s0: all_gather(s0, 'tensor').sum(axis=0)  115 us
    all_gather x1, waiting for transfers between devices, local(): head_rows = lax.all_gather(head, 'seq', axis=1, tiled=True)  53.4 us
    all_gather x1, waiting for transfers between devices, local(): value_piece = lax.all_gather(prompt_value_slots, 'seq', axis=0, tiled=True)  36.4 us
    all_gather x1, waiting for transfers between devices, local(): key_piece = lax.all_gather(prompt_key_slots, 'seq', axis=0, tiled=True)  24.7 us
    psum x1, blocking collectives, local(): lax.psum(adapter_portion.astype(jnp.bfloat16), 'tensor').astype(jnp.float32)  18.2 us
    dot_general x1, matrix products, local(): jnp.einsum('thd,khd->htk', queries, keys_flat, preferred_element_type=jnp...  18 us
    pmax x1, blocking collectives, local(): whole_max = lax.pmax(local_max, 'tensor')  17.4 us
    reduce_sum x1, other arithmetic, local(): totals = totals * rescale + jnp.sum(weights, axis=-1)  15.2 us
  transfers between devices with their start and end apart: 4, of which 4 were waited for; matrix products, arithmetic and copies ran while one was open for 15% of the time, Pallas kernels for 0%

profile of v1, /device:TPU:2, one launch (start us, length us, event | category | flops | bytes accessed | tf_op | source)
XLA Modules:
  0.0 450.4 jit_solution(6196841426294762335)
XLA Ops:
  7.2 0.7 all-gather.6.cloned.1.call-update
  7.9 0.0 all-gather.8.cloned.1.call-start
  8.0 0.7 all-gather.8.cloned.1.call-update
  8.7 0.0 all-gather.12.cloned.1.call-start
  8.7 0.7 dynamic_slice.3
  9.4 0.1 broadcast_in_dim.114
  9.5 0.1 eq.78
  9.6 0.7 convert_element_type.57
  10.3 5.1 %slice_bitcast_fusion = (bf16[384,3072]{0,1:T(8,128)(2,1)}, bf16[384,3072]{0,1:T(8,128)(2,1)}) fusion(bf16[3,3072,384]{2,1,0:T(8,128)(2,1)} %param.16), kind=kLoop, calls=%fused_computation.29 | loop fusion | bytes 9437184 | tf_op jit(solution)/shard_map/dot_general | solution.py:73
  15.4 4.3 copy.69
  19.7 4.3 copy.66
  24.0 0.1 select_reduce_fusion.5
  24.1 1.8 fusion.5
  25.9 0.3 multiply_cosine_fusion
  26.2 3.2 fusion.15
  29.4 0.1 copy-done.5
  29.6 0.9 fusion.17
  30.5 0.1 subtract_convert_fusion
  30.6 0.1 concatenate.32
  30.7 0.2 copy.67
  31.0 0.1 concatenate.33
  31.1 0.2 copy.68
  31.3 0.1 concatenate.35
  31.5 0.9 copy.70
  32.4 0.1 concatenate.36
  32.5 0.9 copy.71
  33.4 1.5 select_reduce_fusion.2
  34.9 0.1 fusion.31
  35.0 0.1 reshape.237
  35.1 0.1 reshape.234
  35.2 3.2 fusion.22
  38.4 0.2 reshape_reshape.3
  38.6 0.3 convolution_bitcast_fusion
  38.9 0.2 copy.77
  39.1 0.1 select_reduce_fusion.3
  39.2 0.1 select_reduce_fusion.6
  39.3 0.1 broadcast_bitcast_fusion.1
  39.4 0.1 broadcast_bitcast_fusion
  39.5 2.8 compare_and_fusion
  42.3 24.7 %all-gather.6.cloned.1.call-done = bf16[64,128,384]{2,1,0:T(8,128)(2,1)} async-done(((bf16[2,128,384]{2,1,0:T(8,128)(2,1)}), bf16[64,128,384]{2,1,0:T(8,128)(2,1)}) %all-gather.6.cloned.1.call-update) | async-done | bytes 6291472 | tf_op jit(solution)/shard_map/all_gather | solution.py:104
  67.0 9.0 %copy.76 = bf16[64,128,384]{1,0,2:T(8,128)(2,1)} copy(bf16[64,128,384]{2,1,0:T(8,128)(2,1)} %all-gather.6.cloned.1.call-done) | data formatting | bytes 12582912 | tf_op jit(solution)/shard_map/all_gather | solution.py:104
  76.0 10.3 %reshape.235 = bf16[8192,4,96]{0,2,1:T(8,128)(2,1)} reshape(bf16[64,128,384]{1,0,2:T(8,128)(2,1)} %copy.76) | data formatting | bytes 12582912 | tf_op jit(solution)/shard_map/reshape | solution.py:119
  86.3 36.4 %all-gather.8.cloned.1.call-done = bf16[64,128,384]{2,1,0:T(8,128)(2,1)} async-done(((bf16[2,128,384]{2,1,0:T(8,128)(2,1)}), bf16[64,128,384]{2,1,0:T(8,128)(2,1)}) %all-gather.8.cloned.1.call-update) | async-done | bytes 6291472 | tf_op jit(solution)/shard_map/all_gather | solution.py:105
  122.7 9.1 %copy.78 = bf16[64,128,384]{1,0,2:T(8,128)(2,1)} copy(bf16[64,128,384]{2,1,0:T(8,128)(2,1)} %all-gather.8.cloned.1.call-done) | data formatting | bytes 12582912 | tf_op jit(solution)/shard_map/all_gather | solution.py:105
  131.8 10.3 %reshape.236 = bf16[8192,4,96]{0,2,1:T(8,128)(2,1)} reshape(bf16[64,128,384]{1,0,2:T(8,128)(2,1)} %copy.78) | data formatting | bytes 12582912 | tf_op jit(solution)/shard_map/reshape | solution.py:120
  142.1 18.0 %select_reduce_fusion = (f32[4,256]{1,0:T(4,128)S(1)}, f32[4,256,8192]{2,1,0:T(8,128)}) fusion(pred[256,8192]{1,0:T(8,128)(4,1)} %compare_and_fusion, bf16[8192,4,96]{0,2,1:T(8,128)(2,1)} %reshape.235, bf16[256,4,48]{0,2,1:T(8,128)(2,1)S(1)} %get-tuple-element.16, bf16[256,4,48]{0,2,1:T(8,128)(2,1)S(1)} %copy-done.7), kind=kOutput, calls=%fused_computation.1 | convolution fusion | flops 1636170752 | bytes 42143744 | tf_op jit(solution)/shard_map/thd,khd->htk/dot_general | solution.py:122
  160.1 15.2 %fusion = f32[4,256]{1,0:T(4,128)S(1)} fusion(f32[4,256,8192]{2,1,0:T(8,128)} %get-tuple-element.27, f32[4,256]{1,0:T(4,128)S(1)} %max.15, pred[256,8192]{1,0:T(8,128)(4,1)S(1)} %copy-done.4), kind=kLoop, calls=%fused_computation.2 | loop fusion | flops 33553408 | bytes 35659776 | tf_op jit(solution)/shard_map/reduce_sum | solution.py:129
  175.4 15.2 %fusion.28 = bf16[4,256,96]{1,2,0:T(8,128)(2,1)S(1)} fusion(bf16[8192,4,96]{0,2,1:T(8,128)(2,1)} %reshape.236, f32[4,256,8192]{2,1,0:T(8,128)} %get-tuple-element.27, f32[4,256]{1,0:T(4,128)S(1)} %max.15, pred[256,8192]{1,0:T(8,128)(4,1)S(1)} %copy-done.4, f32[4,256,96]{1,2,0:T(8,128)S(1)} %copy.77, f32[4,256]{1,0:T(4,128)S(1)} %get-tuple-element.8, ...), kind=kOutput, calls=%fused_computation.40 | convolution fusion | flops 1644560384 | bytes 42545152 | tf_op jit(solution)/shard_map/htk,khd->htd/dot_general | solution.py:130
  190.7 2.2 convolution_convert_fusion
  192.9 0.0 all-gather.10.cloned.1.call-start
  193.0 0.5 all-gather.10.cloned.1.call-update
  193.6 0.1 convolution_convert_fusion.1
  193.7 18.2 %psum.21 = bf16[256,16]{0,1:T(8,128)(2,1)S(1)} all-reduce(bf16[256,16]{0,1:T(8,128)(2,1)S(1)} %convolution_convert_fusion.1), channel_id=1, replica_groups=mesh['seq'=32,'tensor'=8] {'tensor'}, use_global_device_ids=true, to_apply=%region_10.11 | all-reduce | flops 4096 | bytes 16384 | tf_op jit(solution)/shard_map/psum | solution.py:145
  211.9 114.7 %all-gather.12.cloned.1.call-done = bf16[2048,3072]{1,0:T(8,128)(2,1)} async-done(((bf16[256,3072]{1,0:T(8,128)(2,1)}), bf16[2048,3072]{1,0:T(8,128)(2,1)}) %all-gather.12.cloned.1.call-update) | async-done | bytes 12582928 | tf_op jit(solution)/shard_map/all_gather | solution.py:142
  326.6 8.8 %reduce_sum.118 = bf16[256,3072]{1,0:T(8,128)(2,1)} reduce(bf16[8,256,3072]{2,1,0:T(8,128)(2,1)} %bitcast.56, bf16[]{:T(256)} %constant.87.clone.1), dimensions={0}, to_apply=%region_9.10 | reduce | flops 5505024 | bytes 14155778 | tf_op jit(solution)/shard_map/reduce_sum | solution.py:142
  335.4 2.9 multiply_reduce_fusion.1
  338.3 0.6 multiply_reduce_fusion
  338.9 3.0 multiply_convert_fusion.1
  341.9 53.4 %all-gather.10.cloned.1.call-done = bf16[2048,3072]{0,1:T(8,128)(2,1)} async-done(((bf16[2048,96]{0,1:T(8,128)(2,1)}), bf16[2048,3072]{0,1:T(8,128)(2,1)}) %all-gather.10.cloned.1.call-update) | async-done | bytes 12582928 | tf_op jit(solution)/shard_map/all_gather | solution.py:153
  395.3 11.9 %fusion.60 = (f32[512]{0:T(512)S(1)}, f32[512,2048]{1,0:T(8,128)}) fusion(bf16[2048,3072]{0,1:T(8,128)(2,1)} %all-gather.10.cloned.1.call-done, bf16[256,3072]{1,0:T(8,128)(2,1)} %get-tuple-element.19, bf16[256,3072]{1,0:T(8,128)(2,1)} %get-tuple-element.18), kind=kOutput, calls=%fused_computation.99 | convolution fusion | flops 6449790464 | bytes 19924992 | tf_op jit(solution)/shard_map/dot_general | solution.py:155
  407.2 17.4 %pmax.7 = f32[512]{0:T(512)S(1)} all-reduce(f32[512]{0:T(512)S(1)} %get-tuple-element.30), channel_id=1, replica_groups=mesh['seq'=32,'tensor'=8] {'tensor'}, use_global_device_ids=true, to_apply=%region_16.17 | all-reduce | flops 512 | bytes 4096 | tf_op jit(solution)/shard_map/pmax | solution.py:163
  424.6 3.6 select_reduce_fusion.1
  428.3 15.0 %all-reduce = (f32[512]{0:T(512)S(1)}, f32[512]{0:T(512)S(1)}) all-reduce(f32[512]{0:T(512)S(1)} %get-tuple-element.3, f32[512]{0:T(512)S(1)} %get-tuple-element.2), channel_id=1, replica_groups=mesh['seq'=32,'tensor'=8] {'tensor'}, use_global_device_ids=true, to_apply=%region_18.19 | all-reduce | flops 1024 | bytes 8192 | tf_op jit(solution)/shard_map/psum | solution.py:165
  443.3 0.6 fusion.59
  (45 shorter events, 0.3 us)
Async XLA Ops:
  7.2 183.5 %copy-start = (bf16[384,3072]{1,0:T(8,128)(2,1)S(1)}, bf16[384,3072]{1,0:T(8,128)(2,1)}, u32[]{:S(2)}) copy-start(bf16[384,3072]{1,0:T(8,128)(2,1)} %param.17) | copy-start | bytes 7077892
  7.2 59.8 %all-gather.6.cloned.1.call-start = ((), (), s32[]{:S(2)}) async-start(), calls=%async_computation | async-start | bytes 6488064 | tf_op jit(solution)/shard_map/all_gather | solution.py:104
  7.9 114.8 %all-gather.8.cloned.1.call-start = ((), (), s32[]{:S(2)}) async-start(), calls=%async_computation.1 | async-start | bytes 6488064 | tf_op jit(solution)/shard_map/all_gather | solution.py:105
  8.7 317.9 %all-gather.12.cloned.1.call-start = ((), (), s32[]{:S(2)}) async-start(), calls=%async_computation.3 | async-start | bytes 14155776 | tf_op jit(solution)/shard_map/all_gather | solution.py:142
  19.7 4.3 copy-start.13
  26.2 3.3 copy-start.1
  26.2 3.4 copy-start.5
  30.6 2.8 copy-start.6
  38.4 0.7 copy-start.12
  131.8 10.3 %copy-start.7 = (bf16[256,4,48]{0,2,1:T(8,128)(2,1)S(1)}, bf16[256,4,48]{0,2,1:T(8,128)(2,1)}, u32[]{:S(2)}) copy-start(bf16[256,4,48]{0,2,1:T(8,128)(2,1)} %copy-done.6) | copy-start | bytes 294916
  142.1 18.0 %copy-start.4 = (pred[256,8192]{1,0:T(8,128)(4,1)S(1)}, pred[256,8192]{1,0:T(8,128)(4,1)}, u32[]{:S(2)}) copy-start(pred[256,8192]{1,0:T(8,128)(4,1)} %compare_and_fusion) | copy-start | bytes 6291460
  190.6 2.9 copy-start.10
  190.6 2.9 copy-start.11
  190.6 2.9 copy-start.9
  192.9 202.4 %all-gather.10.cloned.1.call-start = ((), (), s32[]{:S(2)}) async-start(), calls=%async_computation.2 | async-start | bytes 12976128 | tf_op jit(solution)/shard_map/all_gather | solution.py:153
  326.6 8.8 %copy-start.8 = (bf16[16,3072]{1,0:T(8,128)(2,1)S(1)}, bf16[16,3072]{1,0:T(8,128)(2,1)}, u32[]{:S(2)}) copy-start(bf16[16,3072]{1,0:T(8,128)(2,1)} %param.19) | copy-start | bytes 294916
  335.4 2.9 copy-start.2
  335.4 2.9 copy-start.3
Sparse Core Ops, SparseCore 0:
  10.6 56.3 all-gather.5
  69.5 53.1 all-gather.7
  193.0 133.4 all-gather.11
  329.0 66.2 all-gather.9
